TPU v7x, 256 devices: a whole 4x4x8 slice. The times are simulated.
256 devices in a mesh: grp: 32 (over z, x), vocab: 8 (over y, core).
Axes of the slice: x: 4, y: 4, z: 8, core: 2. Of those that a mesh axis runs over, the one named last changes fastest.
Arguments:
- final_hidden: bfloat16 [8192, 2048], P('grp')
- norm_gain: float32 [2048], replicated, may hold values from 0.5 to 1.5
- head_weight: bfloat16 [50176, 2048], P(('vocab', 'grp'))
- token_ids: int32 [8192], replicated, may hold values from 0 to 50175
- group_lengths: int32 [32], replicated, may hold values from 1 to 256, as said below
- segment_ids: int32 [8192], P('grp'), may hold values from 0 to 3, as said below
- continues: int32 [32], replicated, may hold values from 0 to 1, as said below
- layer_input: bfloat16 [8192, 2048], P('grp')
- key_weight: bfloat16 [2048, 2048], P(None, 'vocab')
- key_gain: float32 [2048], P('vocab'), may hold values from 0.5 to 1.5
- positions: int32 [8192], P('grp'), may hold values from 0 to 16383
- key_rows: int32 [800], P('grp'), may hold values from 0 to 255, as said below
Outputs:
- token_logprob: float32 [8192], P('grp')
- token_entropy: float32 [8192], P('grp')
- request_mean: float32 [128], P('grp')
- keys: bfloat16 [800, 2048], P('grp', 'vocab')
Inputs may be any that keep to these rules, and one draw needn't show every extreme that they name: For every g below 16, group_lengths[g] + group_lengths[g + 16] <= 320; groups 0 and 16 reach that bound, and group 0 fills all 256 slots. `segment_ids`: never falls along a group's slots. `continues`: 0 for odd g, 1 for g = 0 and for g = 30. `key_rows`: each entry is below its group's length.
All inputs are finite; a program needn't handle non-finite values.
Results may differ from a plain program's by a relative error of at most 0.0071.
Values may be sent and summed in bfloat16 or wider, within the bound.
A program may use at most 128 MiB of HBM per device.

v0:
```python
import jax
import jax.numpy as jnp
from jax import lax
from jax.sharding import PartitionSpec as P

HD = 128
SEGS = 4


NORM_EPS = 1e-06
ROPE_BASE = 500000.0


def joined_2(part, axis, combine):
    gathered = jax.tree.map(lambda a: lax.all_gather(a, axis), part)

    def take(source):
        return jax.tree.map(lambda a: lax.dynamic_index_in_dim(a, source, 0, False), gathered)

    return lax.fori_loop(
        1, lax.axis_size(axis), lambda source, state: combine(state, take(source)), take(0)
    )


def swapped(array, axis, apart):
    return lax.ppermute(array, axis, [(i, i ^ 1 << apart) for i in range(lax.axis_size(axis))])


def normalize(hidden, gain):
    widened = hidden.astype(jnp.float32)
    meansq = jnp.mean(widened * widened, axis=-1, keepdims=True)
    return (widened * lax.rsqrt(meansq + NORM_EPS) * gain).astype(jnp.bfloat16)


def logit_block(left, right):
    product = lax.dot_general(
        left, right, (((1,), (1,)), ((), ())), preferred_element_type=jnp.float32
    )
    return lax.optimization_barrier(product.astype(jnp.bfloat16)).astype(jnp.float32)


def block_stats(logits, targets, columns):
    highest = jnp.max(logits, axis=1)
    shifted = jnp.exp(logits - highest[:, None])
    expsum = jnp.sum(shifted, axis=1)
    moment = jnp.sum(shifted * logits, axis=1)
    picked = jnp.sum(jnp.where(columns[None, :] == targets[:, None], logits, 0.0), axis=1)
    return (highest, expsum, moment, picked)


def combine_stats(first, second):
    highest = jnp.maximum(first[0], second[0])
    left_scale = jnp.exp(first[0] - highest)
    right_scale = jnp.exp(second[0] - highest)
    return (
        highest,
        first[1] * left_scale + second[1] * right_scale,
        first[2] * left_scale + second[2] * right_scale,
        first[3] + second[3],
    )


def empty_stats(count):
    zeros = jnp.zeros((count,), jnp.float32)
    return (jnp.full((count,), -jnp.inf, jnp.float32), zeros, zeros, zeros)


def finish_stats(stats):
    merged = joined_2(stats, "vocab", combine_stats)
    logsum = merged[0] + jnp.log(merged[1])
    return (merged[3] - logsum, logsum - merged[2] / merged[1])


def rotate(values, places):
    count = values.shape[0]
    heads = values.shape[1] // HD
    half = HD // 2
    shaped = values.reshape(count, heads, HD)
    steps = jnp.arange(half).astype(jnp.float32)
    freqs = jnp.exp(-(2.0 * steps / HD) * jnp.log(jnp.float32(ROPE_BASE)))
    angles = places[:, None] * freqs[None, :]
    cosine = jnp.cos(angles)[:, None, :]
    sine = jnp.sin(angles)[:, None, :]
    first = shaped[..., :half]
    second = shaped[..., half:]
    turned = jnp.concatenate(
        [first * cosine - second * sine, second * cosine + first * sine], axis=-1
    )
    return turned.reshape(count, heads * HD)


def local(
    final_hidden,
    norm_gain,
    head_weight,
    token_ids,
    group_lengths,
    segment_ids,
    continues,
    layer_input,
    key_weight,
    key_gain,
    positions,
    key_rows,
):
    row_cap = final_hidden.shape[0]
    groups = lax.axis_size("grp")
    shards = lax.axis_size("vocab")
    group_here = lax.axis_index("grp")
    shard_here = lax.axis_index("vocab")
    local_vocab = head_weight.shape[0]
    shard_vocab = local_vocab * groups
    shard_start = shard_here * shard_vocab
    normed = normalize(final_hidden, norm_gain)
    my_len = group_lengths[group_here]
    slots = jnp.arange(row_cap, dtype=jnp.int32)
    live = slots < my_len
    my_ids = lax.dynamic_slice_in_dim(token_ids, group_here * row_cap, row_cap)
    piece = lax.all_gather(head_weight, "grp", axis=0, tiled=True)
    logits = logit_block(normed, piece)
    columns = shard_start + jnp.arange(piece.shape[0], dtype=jnp.int32)
    stats = combine_stats(empty_stats(normed.shape[0]), block_stats(logits, my_ids, columns))
    logprob, entropy = finish_stats(stats)
    logprob = jnp.where(live, logprob, 0.0)
    entropy = jnp.where(live, entropy, 0.0)
    labels = jnp.arange(SEGS, dtype=jnp.int32)
    member = (segment_ids[:, None] == labels[None, :]) & live[:, None]
    sums = jnp.sum(jnp.where(member, logprob[:, None], 0.0), axis=0)
    counts = jnp.sum(member.astype(jnp.float32), axis=0)
    partner_sums, partner_counts = swapped((sums, counts), "grp", 0)
    is_even = group_here % 2 == 0
    partner = jnp.bitwise_xor(group_here, 1)
    joined = jnp.where(is_even, continues[group_here], continues[partner]) == 1
    my_last = jnp.take(segment_ids, my_len - 1)
    partner_last = jnp.max(jnp.where(partner_counts > 0, labels, 0))
    extra_sum = jnp.where(is_even, partner_sums[0], jnp.take(partner_sums, partner_last))
    extra_count = jnp.where(is_even, partner_counts[0], jnp.take(partner_counts, partner_last))
    target_slot = jnp.where(is_even, my_last, 0)
    update = joined & (labels == target_slot)
    total_sum = sums + jnp.where(update, extra_sum, 0.0)
    total_count = counts + jnp.where(update, extra_count, 0.0)
    request_mean = total_sum / jnp.maximum(total_count, 1.0)
    chosen = jnp.take(layer_input, key_rows, axis=0)
    projected = jnp.dot(chosen, key_weight, preferred_element_type=jnp.float32)
    local_squares = jnp.sum(projected * projected, axis=1)
    all_squares = lax.psum(local_squares, "vocab")
    key_width = key_weight.shape[1] * shards
    scale = jnp.sqrt(all_squares / key_width + NORM_EPS)
    normal_keys = projected / scale[:, None] * key_gain
    places = jnp.take(positions, key_rows).astype(jnp.float32)
    keys = rotate(normal_keys, places).astype(jnp.bfloat16)
    return (logprob, entropy, request_mean, keys)


def solution(mesh):
    in_specs = (
        P("grp", None),
        P(),
        P(("vocab", "grp"), None),
        P(),
        P(),
        P("grp"),
        P(),
        P("grp", None),
        P(None, "vocab"),
        P("vocab"),
        P("grp"),
        P("grp"),
    )
    out_specs = (P("grp"), P("grp"), P("grp"), P("grp", "vocab"))
    return jax.shard_map(local, mesh=mesh, in_specs=in_specs, out_specs=out_specs, check_vma=False)
```

profile of v0, /device:TPU:1, one launch (start us, length us, event | category | flops | bytes accessed | tf_op | source)
XLA Modules:
  0.0 303.3 jit_solution(6285765216668916315)
XLA Ops:
  7.2 0.7 all-gather.9.cloned.1.call-update
  7.9 1.2 dynamic_slice.65
  10.5 1.3 fusion.19
  13.1 1.3 dynamic-slice.6
  15.0 0.7 compare_select_fusion
  15.7 0.6 gather_fusion
  16.4 1.4 gather_fusion.1
  17.7 0.7 select_convert_fusion
  18.4 1.7 multiply_reduce_fusion
  20.1 15.0 %psum.7 = f32[25]{0:T(128)S(1)} all-reduce(f32[25]{0:T(128)S(1)} %get-tuple-element.309), channel_id=1, replica_groups=mesh['grp'=32,'vocab'=8] {'vocab'}, use_global_device_ids=true, to_apply=%region_11.12 | all-reduce | flops 25 | bytes 200 | tf_op jit(solution)/shard_map/psum | solution.py:146
  35.1 0.8 divide_multiply_fusion
  36.3 0.6 copy.20
  36.9 0.8 dynamic_slice.69
  37.6 0.7 iota_compare_fusion.1
  38.3 1.5 fusion.4
  39.9 164.1 %all-gather.9.cloned.1.call-done = bf16[32,196,2048]{2,1,0:T(8,128)(2,1)} async-done(((bf16[1,196,2048]{2,1,0:T(8,128)(2,1)}), bf16[32,196,2048]{2,1,0:T(8,128)(2,1)}) %all-gather.9.cloned.1.call-update) | async-done | bytes 25690128 | tf_op jit(solution)/shard_map/all_gather | solution.py:119
  204.0 24.0 %reshape.276 = bf16[6272,2048]{1,0:T(8,128)(2,1)} reshape(bf16[32,196,2048]{2,1,0:T(8,128)(2,1)} %all-gather.9.cloned.1.call-done) | data formatting | bytes 51380224
  228.0 13.9 %convolution_convert_fusion = bf16[256,6272]{1,0:T(8,128)(2,1)} fusion(bf16[6272,2048]{1,0:T(8,128)(2,1)} %reshape.276, bf16[256,2048]{1,0:T(8,128)(2,1)S(1)} %copy-done.1, f32[2048]{0:T(1024)S(1)} %copy-done.4, f32[256]{0:T(256)S(1)} %add_rsqrt_fusion), kind=kOutput, calls=%fused_computation.13 | convolution fusion | flops 6580371456 | bytes 29959168 | tf_op jit(solution)/shard_map/dot_general | solution.py:36
  241.9 2.4 reduce_max.27
  244.3 11.4 %all-gather.3 = f32[8,1,256]{2,1,0:T(1,128)S(1)} all-gather(f32[1,1,256]{2,1,0:T(1,128)S(1)} %bitcast.65), channel_id=2, replica_groups=mesh['grp'=32,'vocab'=8] {'vocab'}, dimensions={0}, use_global_device_ids=true | all-gather | bytes 9216 | tf_op jit(solution)/shard_map/all_gather | solution.py:15
  255.7 3.9 %fusion.2 = (f32[256]{0:T(256)S(1)}, f32[256]{0:T(256)S(1)}, f32[256]{0:T(256)S(1)}) fusion(bf16[256,6272]{1,0:T(8,128)(2,1)} %convolution_convert_fusion, f32[256]{0:T(256)S(1)} %reduce_max.32, s32[256]{0:T(256)S(1)} %dynamic_slice.69, s32[6272]{0:T(1024)S(1)} %iota_add_fusion), kind=kLoop, calls=%fused_computation.16 | loop fusion | flops 12844288 | bytes 3241472 | tf_op jit(solution)/shard_map/reduce_sum | solution.py:46
  259.6 8.1 %all-gather.4 = f32[8,1,256]{2,1,0:T(1,128)S(1)} all-gather(f32[1,1,256]{2,1,0:T(1,128)S(1)} %bitcast.67), channel_id=1, replica_groups=mesh['grp'=32,'vocab'=8] {'vocab'}, dimensions={0}, use_global_device_ids=true | all-gather | bytes 9216 | tf_op jit(solution)/shard_map/all_gather | solution.py:15
  267.8 9.5 %all-gather.5 = f32[8,1,256]{2,1,0:T(1,128)S(1)} all-gather(f32[1,1,256]{2,1,0:T(1,128)S(1)} %bitcast.66), channel_id=1, replica_groups=mesh['grp'=32,'vocab'=8] {'vocab'}, dimensions={0}, use_global_device_ids=true | all-gather | bytes 9216 | tf_op jit(solution)/shard_map/all_gather | solution.py:15
  277.2 8.1 %all-gather.6 = f32[8,1,256]{2,1,0:T(1,128)S(1)} all-gather(f32[1,1,256]{2,1,0:T(1,128)S(1)} %bitcast.64), channel_id=3, replica_groups=mesh['grp'=32,'vocab'=8] {'vocab'}, dimensions={0}, use_global_device_ids=true | all-gather | bytes 9216 | tf_op jit(solution)/shard_map/all_gather | solution.py:15
  285.4 0.8 while.24
  286.1 1.2 subtract_select_fusion
  287.4 0.1 select_reduce_fusion
  287.6 1.5 collective-permute-start.1
  289.1 1.0 collective-permute-done.1
  290.1 0.6 fusion.15
  292.7 0.7 fusion.17
  296.0 0.5 maximum_divide_fusion
  (75 shorter events, 1.1 us)
Async XLA Ops:
  7.2 8.6 %copy-start = (bf16[256,2048]{1,0:T(8,128)(2,1)S(1)}, bf16[256,2048]{1,0:T(8,128)(2,1)}, u32[]{:S(2)}) copy-start(bf16[256,2048]{1,0:T(8,128)(2,1)} %param.21) | copy-start | bytes 3145732
  7.2 196.8 %all-gather.9.cloned.1.call-start = ((), (), s32[]{:S(2)}) async-start(), calls=%async_computation | async-start | bytes 27033600 | tf_op jit(solution)/shard_map/all_gather | solution.py:119
  39.8 188.1 %copy-start.1 = (bf16[256,2048]{1,0:T(8,128)(2,1)S(1)}, bf16[256,2048]{1,0:T(8,128)(2,1)}, u32[]{:S(2)}) copy-start(bf16[256,2048]{1,0:T(8,128)(2,1)} %param.14) | copy-start | bytes 3145732
  39.8 188.1 %copy-start.4 = (f32[2048]{0:T(1024)S(1)}, f32[2048]{0:T(1024)}, u32[]{:S(2)}) copy-start(f32[2048]{0:T(1024)} %param.15) | copy-start | bytes 24580
  241.9 45.5 %copy-start.3 = (s32[256]{0:T(256)S(1)}, s32[256]{0:T(256)}, u32[]{:S(2)}) copy-start(s32[256]{0:T(256)} %param.19) | copy-start | bytes 3076
  287.4 9.1 %copy-start.2 = (f32[256]{0:T(256)}, f32[256]{0:T(256)S(1)}, u32[]{:S(2)}) copy-start(f32[256]{0:T(256)S(1)} %get-tuple-element.298) | copy-start | bytes 3076
  287.5 5.2 %collective-permute-start = (f32[4]{0:T(128)S(1)}, f32[4]{0:T(128)S(1)}, u32[]{:S(2)}, u32[]{:S(2)}) collective-permute-start(f32[4]{0:T(128)S(1)} %get-tuple-element.267), channel_id=1, source_target_pairs={{0,8},{8,0},{16,24},{24,16},{32,40},{40,32},{48,56},{56,48},{64,72... | collective-permute-start | bytes 56 | tf_op jit(solution)/shard_map/ppermute | solution.py:26
  287.6 2.5 collective-permute-start.1
Sparse Core Ops, SparseCore 0:
  10.6 193.3 all-gather.8
where the time goes:
time: 304 us; the launch traced here: 303 us
  waiting for transfers between devices  166 us (55%)
  blocking collectives  52.1 us (17%)
  local copies, waits for them, and re-layouts  32.1 us (11%)
  between operations  22 us (7%)
  matrix products  15.6 us (5%)
  other arithmetic  13.8 us (5%)
    all_gather x1, waiting for transfers between devices, local(): piece = lax.all_gather(head_weight, 'grp', axis=0, tiled=True)  164 us
    all_gather x4, blocking collectives, joined_2(): gathered = jax.tree.map(lambda a: lax.all_gather(a, axis), part)  37.1 us
    unnamed x17, local copies, waits for them, and re-layouts  24.7 us
    psum x1, blocking collectives, local(): all_squares = lax.psum(local_squares, 'vocab')  15 us
    dot_general x1, matrix products, logit_block(): lax.dot_general(left, right, (((1,), (1,)), ((), ())), preferred_element_...  13.9 us
  transfers between devices with their start and end apart: 3, of which 2 were waited for; matrix products, arithmetic and copies ran while one was open for 5% of the time, Pallas kernels for 0%

commit v1 on v0

v1 whole, which is shorter than its diff:
```python
import jax
import jax.numpy as jnp
import numpy as np
from jax import lax
from jax.experimental import pallas as pl
from jax.experimental.pallas import tpu as pltpu
from jax.sharding import PartitionSpec as P

HD = 128
SEGS = 4
NORM_EPS = 1e-06
ROPE_BASE = 500000.0

NX, NY, NZ = 4, 4, 8
ROWS = 128
BOTH = 256
DIM = 2048
WROWS = 196
WHALF = DIM // 2
ACOLS = 512
SCOLS = (DIM - ACOLS) // NY
KROWS = 25
KPAD = 32
MESH = pl.DeviceIdType.MESH

TWO_PI_1 = 6.28125
TWO_PI_2 = float(np.float32(round((2 * np.pi - TWO_PI_1) * 2**20) / 2**20))
TWO_PI_3 = float(2 * np.pi - TWO_PI_1 - TWO_PI_2)


def place_of(d):
    return {0: (0, 0), 4: (0, 1), 1: (1, 0), 7: (1, 1), 2: (2, 0), 6: (2, 1), 3: (3, 0), 5: (3, 1)}[d]


def merged(maxes, sums, moments, picks):
    top = jnp.max(maxes, axis=0, keepdims=True)
    scale = jnp.exp(maxes - top)
    return (
        top,
        jnp.sum(sums * scale, axis=0, keepdims=True),
        jnp.sum(moments * scale, axis=0, keepdims=True),
        jnp.sum(picks, axis=0, keepdims=True),
    )


def kernel(
    hidden, weight, layer_input, key_weight,
    gain, tokens, lengths, segments, continues, key_gain, positions, key_rows, freqs,
    logprob_out, entropy_out, mean_out, keys_out,
    raw, held, wts, lin, kwt, toks, acc, gathered, part, parts,
    squares, all_squares, pair_own, pair_got,
    local_sems, send_sems, recv_sems,
):
    grp = lax.axis_index("grp")
    voc = lax.axis_index("vocab")
    x, z = lax.rem(grp, NX), lax.div(grp, NX)
    y, c = lax.div(voc, 2), lax.rem(voc, 2)

    def device(xx, yy, zz, cc):
        return (zz * NX + xx, yy * 2 + cc)

    def up(d):
        return device(x, y, lax.rem(z + d, NZ), c)

    x_up = device(lax.rem(x + 1, NX), y, z, c)
    x_down = device(lax.rem(x + NX - 1, NX), y, z, c)
    y_up = device(x, lax.rem(y + 1, NY), z, c)
    y_down = device(x, lax.rem(y + NY - 1, NY), z, c)
    sibling = device(x, y, z, 1 - c)
    partner = device(x + 1 - 2 * lax.rem(x, 2), y, z, c)
    voc_peers = [(grp, lax.rem(voc + d, 8)) for d in range(1, 8)]

    ids = {}

    def remote(name, src, dst, to):
        number = ids.setdefault(name, len(ids))
        return pltpu.make_async_remote_copy(
            src_ref=src, dst_ref=dst, send_sem=send_sems.at[number], recv_sem=recv_sems.at[number],
            device_id=to, device_id_type=MESH,
        )

    sent = []

    def send(name, src, dst, to):
        copy = remote(name, src, dst, to)
        copy.start()
        sent.append(copy)

    def receive(name, dst, to):
        remote(name, dst, dst, to).wait_recv()

    local_copies = [
        pltpu.make_async_copy(hidden.at[pl.ds(pl.multiple_of(c * ROWS, ROWS), ROWS)], raw, local_sems.at[0]),
        pltpu.make_async_copy(weight, wts.at[0], local_sems.at[1]),
        pltpu.make_async_copy(layer_input, lin, local_sems.at[2]),
        pltpu.make_async_copy(key_weight, kwt, local_sems.at[3]),
    ]
    for copy in local_copies:
        copy.start()

    barrier = pltpu.get_barrier_semaphore()
    peers = [up(d) for d in range(1, NZ)] + voc_peers + [x_up, x_down]
    for peer in peers:
        pl.semaphore_signal(barrier, inc=1, device_id=peer, device_id_type=MESH)
    pl.semaphore_wait(barrier, len(peers))

    left, right = pl.ds(0, WHALF), pl.ds(WHALF, WHALF)
    send("w+L", weight.at[:, left], wts.at[1, :, left], x_up)
    send("w-R", weight.at[:, right], wts.at[2, :, right], x_down)
    send("w+R", weight.at[:, right], wts.at[1, :, right], x_up)
    send("w-L", weight.at[:, left], wts.at[2, :, left], x_down)
    send("w0", weight, wts.at[4], sibling)

    def to_sibling(slot, cols, name):
        send("s" + name, wts.at[slot, :, cols], wts.at[4 + slot, :, cols], sibling)

    def from_sibling(slot, cols, name):
        receive("s" + name, wts.at[4 + slot, :, cols], sibling)

    local_copies[0].wait()
    total = jnp.zeros((ROWS, HD), jnp.float32)
    for j in range(DIM // HD):
        block = raw[:, j * HD:(j + 1) * HD].astype(jnp.float32)
        total = total + block * block
    inverse = lax.rsqrt(jnp.sum(total, axis=1, keepdims=True) / DIM + NORM_EPS)
    for j in range(DIM // HD):
        block = raw[:, j * HD:(j + 1) * HD].astype(jnp.float32)
        held[0, 0:ROWS, j * HD:(j + 1) * HD] = (block * inverse * gain[j:j + 1, :]).astype(jnp.bfloat16)

    def rows_of(d, cols, first=0, count=ROWS):
        pair, half = place_of(d)
        return held.at[pair, pl.ds(half * ROWS + first, count), cols]

    def share(yy):
        return pl.ds(pl.multiple_of(ACOLS + SCOLS * lax.rem(yy, NY), HD), SCOLS)

    alone = pl.ds(0, ACOLS)
    LAST = {("S", "+"): 3, ("S", "-"): 4, ("A", "+"): 4, ("A", "-"): 3}

    def away(way, k):
        return (NZ - k) % NZ if way == "+" else k

    def z_send(kind, way, k):
        cols = alone if kind == "A" else share(y)
        send(
            f"z{kind}{way}{k}", rows_of(away(way, k - 1), cols), rows_of(away(way, k), cols),
            up(1) if way == "+" else up(NZ - 1),
        )

    def z_receive(kind, k):
        for way in "+-":
            if k > LAST[kind, way]:
                continue
            d = away(way, k)
            cols = alone if kind == "A" else share(y)
            receive(f"z{kind}{way}{k}", rows_of(d, cols), up(1))
            if k < LAST[kind, way]:
                z_send(kind, way, k + 1)
            if kind == "S":
                send(f"y+{d}", rows_of(d, cols), rows_of(d, cols), y_up)
                send(f"y-{d}", rows_of(d, cols), rows_of(d, cols), y_down)

    def groups_at(k):
        return sorted({away("+", k), away("-", k)})

    half_rows = ROWS // 2

    def y_receive(k):
        for d in groups_at(k):
            below, above = share(y + NY - 1), share(y + 1)
            receive(f"y+{d}", rows_of(d, below), y_up)
            ref = rows_of(d, below, 0, half_rows)
            send(f"yf+{d}", ref, ref, y_up)
            receive(f"y-{d}", rows_of(d, above), y_down)
            ref = rows_of(d, above, half_rows, half_rows)
            send(f"yf-{d}", ref, ref, y_down)

    def y_finish(k):
        for d in groups_at(k):
            across = share(y + 2)
            receive(f"yf+{d}", rows_of(d, across, 0, half_rows), y_up)
            receive(f"yf-{d}", rows_of(d, across, half_rows, half_rows), y_down)

    for kind in "SA":
        for way in "+-":
            z_send(kind, way, 1)

    row_ids = lax.broadcasted_iota(jnp.int32, (KPAD, BOTH), 0)
    col_ids = lax.broadcasted_iota(jnp.int32, (KPAD, BOTH), 1)
    wanted = jnp.zeros((KPAD, BOTH), jnp.int32)
    for i in range(KROWS):
        wanted = jnp.where(row_ids == i, key_rows[i], wanted)
    picks = jnp.where(col_ids == wanted, 1.0, 0.0)
    local_copies[2].wait()
    local_copies[3].wait()
    chosen = jnp.dot(picks.astype(jnp.bfloat16), lin[...], preferred_element_type=jnp.float32)
    projected = jnp.dot(chosen.astype(jnp.bfloat16), kwt[...], preferred_element_type=jnp.float32)
    squares[...] = jnp.broadcast_to(jnp.sum(projected * projected, axis=1, keepdims=True), (KPAD, HD))
    for i, peer in enumerate(voc_peers):
        send(f"k{i + 1}", squares, all_squares.at[i + 1], peer)

    for p in range(4):
        acc[p, 0:1, :] = jnp.full((1, BOTH), -jnp.inf, jnp.float32)
        acc[p, 1:8, :] = jnp.zeros((7, BOTH), jnp.float32)
        for half, d in enumerate([d for d in (0, 4, 1, 7, 2, 6, 3, 5) if place_of(d)[0] == p]):
            row = (lax.rem(z + d, NZ) * NX + x) * 2 + c
            toks[p, 0:1, half * ROWS:(half + 1) * ROWS] = tokens[pl.ds(row, 1), :]

    def chunk(p, w):
        other, turn = lax.div(w, 4), lax.rem(w, 4)
        shift = jnp.where(turn == 0, 0, jnp.where(turn == 1, 3, jnp.where(turn == 2, 1, 2)))
        first = (y * 2 + lax.rem(c + other, 2)) * (WROWS * NX * NZ) + (z * NX + lax.rem(x + shift, NX)) * WROWS
        logits = lax.dot_general(
            wts[w], held[p], (((1,), (1,)), ((), ())), preferred_element_type=jnp.float32
        ).astype(jnp.bfloat16).astype(jnp.float32)
        old = acc[p, 0:1, :]
        top = jnp.maximum(old, jnp.max(logits, axis=0, keepdims=True))
        shifted = jnp.exp(logits - top)
        scale = jnp.exp(old - top)
        hit = lax.broadcasted_iota(jnp.int32, (WROWS, BOTH), 0) == toks[p, 0:1, :] - first
        acc[p, 0:1, :] = top
        acc[p, 1:2, :] = acc[p, 1:2, :] * scale + jnp.sum(shifted, axis=0, keepdims=True)
        acc[p, 2:3, :] = acc[p, 2:3, :] * scale + jnp.sum(shifted * logits, axis=0, keepdims=True)
        acc[p, 3:4, :] = acc[p, 3:4, :] + jnp.sum(jnp.where(hit, logits, 0.0), axis=0, keepdims=True)

    def run(start, pairs, blocks, slot_of):
        def step(i, carry):
            chunk(start + lax.div(i, blocks), slot_of(lax.rem(i, blocks)))
            return carry
        lax.fori_loop(0, pairs * blocks, step, 0)

    def own_slots(i):
        return 4 * i

    def near_slots(i):
        return 1 + lax.rem(i, 2) + 4 * lax.div(i, 2)

    def most_slots(i):
        return i + lax.div(i, 3)

    def far_slots(i):
        return 3 + 4 * i

    z_receive("S", 1)
    z_receive("A", 1)

    for i in range(7):
        receive(f"k{i + 1}", all_squares.at[i + 1], sibling)
    square_sum = squares[...]
    for i in range(7):
        square_sum = square_sum + all_squares[i + 1]
    spread = jnp.sqrt(square_sum / (HD * 16) + NORM_EPS)
    places_row = jnp.concatenate([positions[0:1, :], positions[1:2, :]], axis=1).astype(jnp.float32)
    places = jnp.sum(picks * places_row, axis=1, keepdims=True)
    angles = places * freqs[0:1, :]
    turns = jnp.floor(angles * (0.5 / np.pi) + 0.5)
    angles = ((angles - turns * TWO_PI_1) - turns * TWO_PI_2) - turns * TWO_PI_3
    lanes = lax.broadcasted_iota(jnp.int32, (KPAD, HD), 1)
    cosine = jnp.cos(angles)
    sine = jnp.sin(angles)
    sine = jnp.where(lanes < HD // 2, -sine, sine)
    for head in range(2):
        values = projected[:, head * HD:(head + 1) * HD] / spread * key_gain[head:head + 1, :]
        turned = values * cosine + pltpu.roll(values, HD // 2, 1) * sine
        keys_out[:, head * HD:(head + 1) * HD] = turned[0:KROWS].astype(jnp.bfloat16)

    def weights_first():
        receive("w+L", wts.at[1, :, left], x_up)
        send("wf+", wts.at[1, :, left], wts.at[3, :, left], x_up)
        receive("w-R", wts.at[2, :, right], x_down)
        send("wf-", wts.at[2, :, right], wts.at[3, :, right], x_down)
        to_sibling(1, left, "+L")
        to_sibling(2, right, "-R")

    def weights_second():
        receive("w+R", wts.at[1, :, right], x_up)
        to_sibling(1, right, "+R")
        receive("w-L", wts.at[2, :, left], x_down)
        to_sibling(2, left, "-L")

    def weights_third():
        receive("wf+", wts.at[3, :, left], x_up)
        to_sibling(3, left, "f+")
        receive("wf-", wts.at[3, :, right], x_down)
        to_sibling(3, right, "f-")

    weights_first()
    y_receive(1)
    z_receive("S", 2)
    z_receive("A", 2)
    y_finish(1)
    local_copies[1].wait()
    receive("w0", wts.at[4], sibling)
    run(1, 1, 2, own_slots)
    y_receive(2)
    z_receive("S", 3)
    z_receive("A", 3)
    y_finish(2)
    run(2, 1, 2, own_slots)
    weights_second()
    y_receive(3)
    z_receive("S", 4)
    z_receive("A", 4)
    from_sibling(1, left, "+L")
    from_sibling(1, right, "+R")
    from_sibling(2, right, "-R")
    from_sibling(2, left, "-L")
    run(1, 2, 4, near_slots)
    y_finish(3)
    run(3, 1, 6, most_slots)
    y_receive(4)
    weights_third()
    y_finish(4)
    run(0, 1, 6, most_slots)
    from_sibling(3, left, "f+")
    from_sibling(3, right, "f-")
    run(0, 4, 2, far_slots)

    for d in range(1, NZ):
        pair, half = place_of(d)
        send(f"a{d}", acc.at[pair, :, pl.ds(half * ROWS, ROWS)], gathered.at[NZ - d], up(d))
    gathered[0] = acc[0, :, 0:ROWS]
    for d in range(1, NZ):
        receive(f"a{d}", gathered.at[NZ - d], up(d))
    stats = merged(*(gathered[:, i, :] for i in range(4)))
    for i in range(4):
        part[i:i + 1, :] = stats[i]
    part[4:8, :] = jnp.zeros((4, ROWS), jnp.float32)
    mine = c * NY + y
    for i, peer in enumerate(voc_peers):
        send(f"v{i + 1}", part, parts.at[mine], peer)
    parts[mine] = part[...]
    for i in range(7):
        source = lax.rem(voc + 7 - i, 8)
        receive(f"v{i + 1}", parts.at[lax.rem(source, 2) * NY + lax.div(source, 2)], sibling)

    lane = lax.broadcasted_iota(jnp.int32, (1, ROWS), 1)
    length = lengths[grp]
    sum_vec = jnp.zeros((1, ROWS), jnp.float32)
    count_vec = jnp.zeros((1, ROWS), jnp.float32)
    last = jnp.zeros((1, 1), jnp.float32)
    for half in range(2):
        top, expsum, moment, picked = merged(*(parts[half * NY:(half + 1) * NY, i, :] for i in range(4)))
        logsum = top + jnp.log(expsum)
        slot = lane + half * ROWS
        live = slot < length
        logprob = jnp.where(live, picked - logsum, 0.0)
        logprob_out[half:half + 1, :] = logprob
        entropy_out[half:half + 1, :] = jnp.where(live, logsum - moment / expsum, 0.0)
        label = segments[half:half + 1, :]
        last = last + jnp.sum(
            jnp.where(slot == length - 1, label.astype(jnp.float32), 0.0), axis=1, keepdims=True
        )
        for s in range(SEGS):
            member = live & (label == s)
            here = jnp.sum(jnp.where(member, logprob, 0.0), axis=1, keepdims=True)
            count = jnp.sum(jnp.where(member, 1.0, 0.0), axis=1, keepdims=True)
            sum_vec = sum_vec + jnp.where(lane == s, here, 0.0)
            count_vec = count_vec + jnp.where(lane == s, count, 0.0)
    pair_own[0:1, :] = sum_vec
    pair_own[1:2, :] = count_vec
    pair_own[2:8, :] = jnp.zeros((6, ROWS), jnp.float32)
    send("p", pair_own, pair_got, partner)
    receive("p", pair_got, partner)
    got_sums = pair_got[0:1, :]
    got_counts = pair_got[1:2, :]
    even = lax.rem(x, 2) == 0
    joined = continues[grp - lax.rem(grp, 2)] == 1
    lane_f = lane.astype(jnp.float32)
    got_last = jnp.max(jnp.where((got_counts > 0) & (lane < SEGS), lane_f, 0.0), axis=1, keepdims=True)
    source = jnp.where(even, 0.0, got_last)
    target = jnp.where(even, last, 0.0)
    extra_sum = jnp.sum(jnp.where(lane_f == source, got_sums, 0.0), axis=1, keepdims=True)
    extra_count = jnp.sum(jnp.where(lane_f == source, got_counts, 0.0), axis=1, keepdims=True)
    update = joined & (lane_f == target)
    total_sum = sum_vec + jnp.where(update, extra_sum, 0.0)
    total_count = count_vec + jnp.where(update, extra_count, 0.0)
    mean_out[...] = (total_sum / jnp.maximum(total_count, 1.0))[:, 0:SEGS]
    for copy in sent:
        copy.wait_send()


MESSAGES = 96


def local(
    final_hidden, norm_gain, head_weight, token_ids, group_lengths, segment_ids, continues,
    layer_input, key_weight, key_gain, positions, key_rows,
):
    steps = np.arange(HD // 2, dtype=np.float64)
    freqs = np.exp(-(2.0 * steps / HD) * np.log(ROPE_BASE)).astype(np.float32)
    freqs = jnp.asarray(np.concatenate([freqs, freqs])[None, :])
    anywhere = pl.BlockSpec(memory_space=pl.ANY)
    vmem = pl.BlockSpec(memory_space=pltpu.VMEM)
    smem = pl.BlockSpec(memory_space=pltpu.SMEM)
    f32, bf16 = jnp.float32, jnp.bfloat16
    logprob, entropy, mean, keys = pl.pallas_call(
        kernel,
        out_shape=(
            jax.ShapeDtypeStruct((2, ROWS), f32),
            jax.ShapeDtypeStruct((2, ROWS), f32),
            jax.ShapeDtypeStruct((1, SEGS), f32),
            jax.ShapeDtypeStruct((KROWS, BOTH), bf16),
        ),
        in_specs=[anywhere] * 4 + [vmem, vmem, smem, vmem, smem, vmem, vmem, smem, vmem],
        out_specs=(vmem,) * 4,
        scratch_shapes=[
            pltpu.VMEM((ROWS, DIM), bf16),
            pltpu.VMEM((4, BOTH, DIM), bf16),
            pltpu.VMEM((8, WROWS, DIM), bf16),
            pltpu.VMEM((2 * ROWS, DIM), bf16),
            pltpu.VMEM((DIM, BOTH), bf16),
            pltpu.VMEM((4, 1, BOTH), jnp.int32),
            pltpu.VMEM((4, 8, BOTH), f32),
            pltpu.VMEM((8, 8, ROWS), f32),
            pltpu.VMEM((8, ROWS), f32),
            pltpu.VMEM((8, 8, ROWS), f32),
            pltpu.VMEM((KPAD, HD), f32),
            pltpu.VMEM((8, KPAD, HD), f32),
            pltpu.VMEM((8, ROWS), f32),
            pltpu.VMEM((8, ROWS), f32),
            pltpu.SemaphoreType.DMA((4,)),
            pltpu.SemaphoreType.DMA((MESSAGES,)),
            pltpu.SemaphoreType.DMA((MESSAGES,)),
        ],
        compiler_params=pltpu.CompilerParams(
            collective_id=0, has_side_effects=True, vmem_limit_bytes=40 * 2**20
        ),
    )(
        final_hidden, head_weight, layer_input, key_weight,
        norm_gain.reshape(DIM // HD, HD), token_ids.reshape(-1, ROWS), group_lengths,
        segment_ids.reshape(2, ROWS), continues, key_gain.reshape(2, HD),
        positions.reshape(2, ROWS), key_rows, freqs,
    )
    return (logprob.reshape(-1), entropy.reshape(-1), mean.reshape(-1), keys)


def solution(mesh):
    in_specs = (
        P("grp", None),
        P(),
        P(("vocab", "grp"), None),
        P(),
        P(),
        P("grp"),
        P(),
        P("grp", None),
        P(None, "vocab"),
        P("vocab"),
        P("grp"),
        P("grp"),
    )
    out_specs = (P("grp"), P("grp"), P("grp"), P("grp", "vocab"))
    return jax.shard_map(local, mesh=mesh, in_specs=in_specs, out_specs=out_specs, check_vma=False)
```

time: 304 us -> 82.4 us (0.27)
  waiting for transfers between devices: 166 us -> 0 us
  Pallas kernels: 0 us -> 68.7 us
  blocking collectives: 52.1 us -> 0 us
  between operations: 22 us -> 0.67 us
  local copies, waits for them, and re-layouts: 32.1 us -> 12.5 us
  matrix products: 15.6 us -> 0 us
  other arithmetic: 13.8 us -> 0 us
    all_gather x1 -> x0, waiting for transfers between devices: 164 us -> none  [local(): piece = lax.all_gather(head_weight, 'grp', axis=0, tiled=True)]
    pallas_call x0 -> x1, Pallas kernels: none -> 68.7 us  [local(): pl.pallas_call(kernel, out_shape=(jax.ShapeDtypeStruct((2, ROWS), f32), j...]
    all_gather x4 -> x0, blocking collectives: 37.1 us -> none  [joined_2(): gathered = jax.tree.map(lambda a: lax.all_gather(a, axis), part)]
    dot_general x2 -> x0, matrix products: 15.6 us -> none  [the longest x1 13.9 us: logit_block(): lax.dot_general(left, right, (((1,), (1,)), ((), ())), preferred_element_...]
    psum x1 -> x0, blocking collectives: 15 us -> none  [local(): all_squares = lax.psum(local_squares, 'vocab')]
    unnamed x17 -> x30, local copies, waits for them, and re-layouts: 24.7 us -> 12.5 us
    reduce_sum x3 -> x0, other arithmetic: 5.52 us -> none  [the longest x1 3.87 us: block_stats(): moment = jnp.sum(shifted * logits, axis=1)]
    dynamic_slice x21 -> x0, local copies, waits for them, and re-layouts: 3.47 us -> none  [the longest x1 1.33 us: local(): joined = jnp.where(is_even, continues[group_here], continues[partner]) == 1]
  transfers between devices with their start and end apart: 3 -> 0, of which waited for: 2 -> 0; matrix products, arithmetic and copies ran while one was open for 5% -> 0% of each run, Pallas kernels for 0% -> 0%
where the time goes in v1:
time: 82.4 us; the launch traced here: 81.9 us
  Pallas kernels  68.7 us (83%)
  local copies, waits for them, and re-layouts  12.5 us (15%)
    pallas_call x1, Pallas kernels, local(): pl.pallas_call(kernel, out_shape=(jax.ShapeDtypeStruct((2, ROWS), f32), j...  68.7 us
    unnamed x30, local copies, waits for them, and re-layouts  12.5 us

profile of v1, /device:TPU:1, one launch (start us, length us, event | category | flops | bytes accessed | tf_op | source)
XLA Modules:
  0.0 81.9 jit_solution(1377603526968659964)
XLA Ops:
  0.6 0.0 copy-start.5
  0.6 0.0 copy-start.6
  0.7 0.7 copy-done.5
  1.3 0.0 copy-done.6
  1.3 0.0 copy-start
  1.3 1.2 %copy-done = bf16[256,2048]{1,0:T(8,128)(2,1)S(1)} copy-done((bf16[256,2048]{1,0:T(8,128)(2,1)S(1)}, bf16[256,2048]{1,0:T(8,128)(2,1)}, u32[]{:S(2)}) %copy-start) | copy-done | bytes 1048600
  2.6 0.0 copy-start.1
  2.6 1.2 %copy-done.1 = bf16[256,2048]{1,0:T(8,128)(2,1)S(1)} copy-done((bf16[256,2048]{1,0:T(8,128)(2,1)S(1)}, bf16[256,2048]{1,0:T(8,128)(2,1)}, u32[]{:S(2)}) %copy-start.1) | copy-done | bytes 1048600
  3.8 0.0 copy-start.2
  3.8 1.2 %copy-done.2 = bf16[2048,256]{1,0:T(8,128)(2,1)S(1)} copy-done((bf16[2048,256]{1,0:T(8,128)(2,1)S(1)}, bf16[2048,256]{1,0:T(8,128)(2,1)}, u32[]{:S(2)}) %copy-start.2) | copy-done | bytes 1048600
  5.0 0.0 copy-start.3
  5.0 1.1 %copy-done.3 = bf16[196,2048]{1,0:T(8,128)(2,1)S(1)} copy-done((bf16[196,2048]{1,0:T(8,128)(2,1)S(1)}, bf16[196,2048]{1,0:T(8,128)(2,1)}, u32[]{:S(2)}) %copy-start.3) | copy-done | bytes 802840
  6.2 0.0 copy-start.4
  6.2 0.8 copy-done.4
  6.9 0.0 copy-start.7
  6.9 0.7 copy-done.7
  7.6 0.0 copy-start.8
  7.6 0.7 copy-done.8
  8.3 0.0 copy-start.9
  8.3 0.7 copy-done.9
  8.9 0.0 copy-start.10
  8.9 0.7 copy-done.10
  9.6 0.0 copy-start.11
  9.6 0.7 copy-done.11
  10.2 0.0 copy-start.12
  10.2 0.7 copy-done.12
  10.9 68.7 %shard_map.156 = (f32[2,128]{1,0:T(2,128)S(1)}, f32[2,128]{1,0:T(2,128)S(1)}, f32[1,4]{1,0:T(1,128)S(1)}, bf16[25,256]{1,0:T(8,128)(2,1)S(1)}) custom-call(bf16[256,2048]{1,0:T(8,128)(2,1)S(1)} %copy-done, bf16[196,2048]{1,0:T(8,128)(2,1)S(1)} %copy-done.3, bf16[256,2048]{1,0:T(8,128)(2,1)S(1)} %copy-done.1, bf16[2048,256]{1,0:T(8,128)(2,1)S(1)} %copy-done.2, ...), custom_call_target="tpu_custom_call" | custom-call | tf_op jit(solution)/shard_map/pallas_call | solution.py:397
  79.6 0.6 copy.21
  80.2 0.6 copy.22
  80.8 0.5 copy.23
  81.3 0.6 copy.24
Async XLA Ops:
  0.6 0.7 copy-start.5
  0.6 0.7 copy-start.6
  1.3 1.2 %copy-start = (bf16[256,2048]{1,0:T(8,128)(2,1)S(1)}, bf16[256,2048]{1,0:T(8,128)(2,1)}, u32[]{:S(2)}) copy-start(bf16[256,2048]{1,0:T(8,128)(2,1)} %hidden.1) | copy-start | bytes 3145732
  2.6 1.2 %copy-start.1 = (bf16[256,2048]{1,0:T(8,128)(2,1)S(1)}, bf16[256,2048]{1,0:T(8,128)(2,1)}, u32[]{:S(2)}) copy-start(bf16[256,2048]{1,0:T(8,128)(2,1)} %layer_input.1) | copy-start | bytes 3145732
  3.8 1.2 %copy-start.2 = (bf16[2048,256]{1,0:T(8,128)(2,1)S(1)}, bf16[2048,256]{1,0:T(8,128)(2,1)}, u32[]{:S(2)}) copy-start(bf16[2048,256]{1,0:T(8,128)(2,1)} %key_weight.1) | copy-start | bytes 3145732
  5.0 1.1 %copy-start.3 = (bf16[196,2048]{1,0:T(8,128)(2,1)S(1)}, bf16[196,2048]{1,0:T(8,128)(2,1)}, u32[]{:S(2)}) copy-start(bf16[196,2048]{1,0:T(8,128)(2,1)} %weight.1) | copy-start | bytes 2408452
  6.2 0.8 copy-start.4
  6.9 0.7 copy-start.7
  7.6 0.7 copy-start.8
  8.3 0.7 copy-start.9
  8.9 0.7 copy-start.10
  9.6 0.7 copy-start.11
  10.2 0.7 copy-start.12

commit v2 on v1

v2 whole, which is shorter than its diff:
```python
import jax
import jax.numpy as jnp
import numpy as np
from jax import lax
from jax.experimental import pallas as pl
from jax.experimental.pallas import tpu as pltpu
from jax.sharding import PartitionSpec as P

HD = 128
SEGS = 4
NORM_EPS = 1e-06
ROPE_BASE = 500000.0

NX, NY, NZ = 4, 4, 8
ROWS = 128
BOTH = 256
DIM = 2048
WROWS = 196
WPIECE = DIM // 4
SHARE = 352
ALONE = DIM - SHARE * NY
KROWS = 25
KPAD = 32
MESH = pl.DeviceIdType.MESH

TWO_PI_1 = 6.28125
TWO_PI_2 = float(np.float32(round((2 * np.pi - TWO_PI_1) * 2**20) / 2**20))
TWO_PI_3 = float(2 * np.pi - TWO_PI_1 - TWO_PI_2)


def place_of(d):
    return (0, 4, 1, 7, 2, 6, 3, 5).index(d)


def merged(maxes, sums, moments, picks):
    top = jnp.max(maxes, axis=0, keepdims=True)
    scale = jnp.exp(maxes - top)
    return (
        top,
        jnp.sum(sums * scale, axis=0, keepdims=True),
        jnp.sum(moments * scale, axis=0, keepdims=True),
        jnp.sum(picks, axis=0, keepdims=True),
    )


def kernel(
    hidden, weight, layer_input, key_weight,
    gain, tokens, lengths, segments, continues, key_gain, positions, key_rows, freqs,
    logprob_out, entropy_out, mean_out, keys_out,
    raw, held, wts, lin, kwt, toks, acc, gathered, part, parts,
    squares, all_squares, partner_segments,
    local_sems, send_sems, recv_sems,
):
    grp = lax.axis_index("grp")
    voc = lax.axis_index("vocab")
    x, z = lax.rem(grp, NX), lax.div(grp, NX)
    y, c = lax.div(voc, 2), lax.rem(voc, 2)

    def device(xx, yy, zz, cc):
        return (zz * NX + xx, yy * 2 + cc)

    def up(d):
        return device(x, y, lax.rem(z + d, NZ), c)

    x_up = device(lax.rem(x + 1, NX), y, z, c)
    x_down = device(lax.rem(x + NX - 1, NX), y, z, c)
    y_up = device(x, lax.rem(y + 1, NY), z, c)
    y_down = device(x, lax.rem(y + NY - 1, NY), z, c)
    sibling = device(x, y, z, 1 - c)
    partner = grp + 1 - 2 * lax.rem(x, 2)
    voc_peers = [(grp, lax.rem(voc + d, 8)) for d in range(1, 8)]

    ids = {}

    def remote(name, src, dst, to):
        number = ids.setdefault(name, len(ids))
        return pltpu.make_async_remote_copy(
            src_ref=src, dst_ref=dst, send_sem=send_sems.at[number], recv_sem=recv_sems.at[number],
            device_id=to, device_id_type=MESH,
        )

    sent = []

    def send(name, src, dst, to):
        copy = remote(name, src, dst, to)
        copy.start()
        sent.append(copy)

    def receive(name, dst, to):
        remote(name, dst, dst, to).wait_recv()

    local_copies = [
        pltpu.make_async_copy(hidden.at[pl.ds(pl.multiple_of(c * ROWS, ROWS), ROWS)], raw, local_sems.at[0]),
        pltpu.make_async_copy(weight, wts.at[0], local_sems.at[1]),
        pltpu.make_async_copy(layer_input, lin, local_sems.at[2]),
        pltpu.make_async_copy(key_weight, kwt, local_sems.at[3]),
    ]
    for copy in local_copies:
        copy.start()

    barrier = pltpu.get_barrier_semaphore()
    partners = [(partner, lax.rem(voc + d, 8)) for d in range(8)]
    other_x = device(lax.rem(x + 3 + 2 * lax.rem(x, 2), NX), y, z, c)
    peers = [up(d) for d in range(1, NZ)] + voc_peers + partners + [other_x]
    for peer in peers:
        pl.semaphore_signal(barrier, inc=1, device_id=peer, device_id_type=MESH)
    pl.semaphore_wait(barrier, len(peers))

    def piece(q):
        return pl.ds(q * WPIECE, WPIECE)

    def own_piece(way, first, count):
        cols = pl.ds(first * WPIECE, count * WPIECE)
        slot, to = (1, x_up) if way == "+" else (2, x_down)
        send(f"w{way}{first}", weight.at[:, cols], wts.at[slot, :, cols], to)

    own_piece("+", 0, 1)
    own_piece("-", 2, 1)

    def to_sibling(slot, first, count):
        cols = pl.ds(first * WPIECE, count * WPIECE)
        send(f"s{slot}{first}", wts.at[slot, :, cols], wts.at[4 + slot, :, cols], sibling)

    def from_sibling(slot, first, count):
        cols = pl.ds(first * WPIECE, count * WPIECE)
        receive(f"s{slot}{first}", wts.at[4 + slot, :, cols], sibling)

    def weights_near(i):
        receive(f"w+{i}", wts.at[1, :, piece(i)], x_up)
        send(f"wf+{i}", wts.at[1, :, piece(i)], wts.at[3, :, piece(i)], x_up)
        receive(f"w-{i + 2}", wts.at[2, :, piece(i + 2)], x_down)
        send(f"wf-{i + 2}", wts.at[2, :, piece(i + 2)], wts.at[3, :, piece(i + 2)], x_down)
        if i == 1:
            to_sibling(1, 0, 2)
            to_sibling(2, 2, 2)

    def weights_rest():
        cols = pl.ds(2 * WPIECE, 2 * WPIECE)
        receive("w+2", wts.at[1, :, cols], x_up)
        to_sibling(1, 2, 2)
        cols = pl.ds(0, 2 * WPIECE)
        receive("w-0", wts.at[2, :, cols], x_down)
        to_sibling(2, 0, 2)

    def weights_far(i):
        receive(f"wf+{i}", wts.at[3, :, piece(i)], x_up)
        to_sibling(3, i, 1)
        receive(f"wf-{i + 2}", wts.at[3, :, piece(i + 2)], x_down)
        to_sibling(3, i + 2, 1)

    local_copies[0].wait()
    total = jnp.zeros((ROWS, HD), jnp.float32)
    for j in range(DIM // HD):
        block = raw[:, j * HD:(j + 1) * HD].astype(jnp.float32)
        total = total + block * block
    inverse = lax.rsqrt(jnp.sum(total, axis=1, keepdims=True) / DIM + NORM_EPS)
    for j in range(DIM // HD):
        block = raw[:, j * HD:(j + 1) * HD].astype(jnp.float32)
        held[0, j * HD:(j + 1) * HD, :] = (block * inverse * gain[j:j + 1, :]).T.astype(jnp.bfloat16)

    def features(d, first, count):
        return held.at[place_of(d), pl.ds(first, count), :]

    def share(yy, first=0):
        return pl.multiple_of(ALONE + SHARE * lax.rem(yy, NY) + first, 16)

    LAST = {("S", "+"): 3, ("S", "-"): 4, ("A", "+"): 4, ("A", "-"): 3}

    def away(way, k):
        return (NZ - k) % NZ if way == "+" else k

    def z_part(kind, d):
        return features(d, 0, ALONE) if kind == "A" else features(d, share(y), SHARE)

    def z_send(kind, way, k):
        send(
            f"z{kind}{way}{k}", z_part(kind, away(way, k - 1)), z_part(kind, away(way, k)),
            up(1) if way == "+" else up(NZ - 1),
        )

    def z_receive(kind, k):
        for way in "+-":
            if k > LAST[kind, way]:
                continue
            d = away(way, k)
            receive(f"z{kind}{way}{k}", z_part(kind, d), up(1))
            if k < LAST[kind, way]:
                z_send(kind, way, k + 1)
        if kind == "S":
            ref = shares(k, share(y), SHARE)
            send(f"y+{k}", ref, ref, y_up)
            send(f"y-{k}", ref, ref, y_down)

    def shares(k, first, count):
        slots = pl.ds(2 * k, 2) if k < 4 else pl.ds(1, 1)
        return held.at[slots, pl.ds(first, count), :]

    half_share = SHARE // 2

    def y_receive(k):
        below, above = y + NY - 1, y + 1
        receive(f"y+{k}", shares(k, share(below), SHARE), y_up)
        ref = shares(k, share(below), half_share)
        send(f"yf+{k}", ref, ref, y_up)
        receive(f"y-{k}", shares(k, share(above), SHARE), y_down)
        ref = shares(k, share(above, half_share), half_share)
        send(f"yf-{k}", ref, ref, y_down)

    def y_finish(k):
        receive(f"yf+{k}", shares(k, share(y + 2), half_share), y_up)
        receive(f"yf-{k}", shares(k, share(y + 2, half_share), half_share), y_down)

    for kind in "SA":
        for way in "+-":
            z_send(kind, way, 1)
    own_piece("+", 1, 1)
    own_piece("-", 3, 1)
    own_piece("+", 2, 2)
    own_piece("-", 0, 2)
    send("w0", weight, wts.at[4], sibling)
    send("g", segments, partner_segments, partners[0])

    row_ids = lax.broadcasted_iota(jnp.int32, (KPAD, BOTH), 0)
    col_ids = lax.broadcasted_iota(jnp.int32, (KPAD, BOTH), 1)
    wanted = jnp.zeros((KPAD, BOTH), jnp.int32)
    for i in range(KROWS):
        wanted = jnp.where(row_ids == i, key_rows[i], wanted)
    picks = jnp.where(col_ids == wanted, 1.0, 0.0)
    local_copies[2].wait()
    local_copies[3].wait()
    chosen = jnp.dot(picks.astype(jnp.bfloat16), lin[...], preferred_element_type=jnp.float32)
    projected = jnp.dot(chosen.astype(jnp.bfloat16), kwt[...], preferred_element_type=jnp.float32)
    squares[...] = jnp.broadcast_to(jnp.sum(projected * projected, axis=1, keepdims=True), (KPAD, HD))
    for i, peer in enumerate(voc_peers):
        send(f"k{i + 1}", squares, all_squares.at[i + 1], peer)

    for p in range(4):
        acc[p, 0:1, :] = jnp.full((1, BOTH), -jnp.inf, jnp.float32)
        acc[p, 1:8, :] = jnp.zeros((7, BOTH), jnp.float32)
        for half, d in enumerate((0, 4, 1, 7, 2, 6, 3, 5)[2 * p:2 * p + 2]):
            row = (lax.rem(z + d, NZ) * NX + x) * 2 + c
            toks[p, 0:1, half * ROWS:(half + 1) * ROWS] = tokens[pl.ds(row, 1), :]

    def chunk(p, w):
        other, turn = divmod(w, 4)
        shift = (0, NX - 1, 1, 2)[turn]
        first = (y * 2 + lax.rem(c + other, 2)) * (WROWS * NX * NZ) + (z * NX + lax.rem(x + shift, NX)) * WROWS
        logits = lax.dot_general(
            wts[w], jnp.concatenate([held[2 * p], held[2 * p + 1]], axis=1),
            (((1,), (0,)), ((), ())), preferred_element_type=jnp.float32
        ).astype(jnp.bfloat16).astype(jnp.float32)
        old = acc[p, 0:1, :]
        top = jnp.maximum(old, jnp.max(logits, axis=0, keepdims=True))
        shifted = jnp.exp(logits - top)
        scale = jnp.exp(old - top)
        hit = lax.broadcasted_iota(jnp.int32, (WROWS, BOTH), 0) == toks[p, 0:1, :] - first
        acc[p, 0:1, :] = top
        acc[p, 1:2, :] = acc[p, 1:2, :] * scale + jnp.sum(shifted, axis=0, keepdims=True)
        acc[p, 2:3, :] = acc[p, 2:3, :] * scale + jnp.sum(shifted * logits, axis=0, keepdims=True)
        acc[p, 3:4, :] = acc[p, 3:4, :] + jnp.sum(jnp.where(hit, logits, 0.0), axis=0, keepdims=True)

    def run(pairs, slots):
        for p in pairs:
            for w in slots:
                chunk(p, w)

    def give(p):
        for half, d in enumerate((0, 4, 1, 7, 2, 6, 3, 5)[2 * p:2 * p + 2]):
            if d:
                send(f"a{d}", acc.at[p, :, pl.ds(half * ROWS, ROWS)], gathered.at[NZ - d], up(d))

    z_receive("S", 1)
    z_receive("A", 1)
    z_receive("S", 2)
    y_receive(1)

    weights_near(0)
    z_receive("A", 2)
    z_receive("S", 3)
    weights_near(1)
    y_finish(1)
    local_copies[1].wait()
    receive("w0", wts.at[4], sibling)
    run((1,), (0, 4))
    y_receive(2)
    z_receive("A", 3)
    z_receive("S", 4)
    y_finish(2)
    y_receive(3)

    for i in range(7):
        receive(f"k{i + 1}", all_squares.at[i + 1], sibling)
    square_sum = squares[...]
    for i in range(7):
        square_sum = square_sum + all_squares[i + 1]
    spread = jnp.sqrt(square_sum / (HD * 16) + NORM_EPS)
    places_row = jnp.concatenate([positions[0:1, :], positions[1:2, :]], axis=1).astype(jnp.float32)
    places = jnp.sum(picks * places_row, axis=1, keepdims=True)
    angles = places * freqs[0:1, :]
    turns = jnp.floor(angles * (0.5 / np.pi) + 0.5)
    angles = ((angles - turns * TWO_PI_1) - turns * TWO_PI_2) - turns * TWO_PI_3
    lanes = lax.broadcasted_iota(jnp.int32, (KPAD, HD), 1)
    cosine = jnp.cos(angles)
    sine = jnp.sin(angles)
    sine = jnp.where(lanes < HD // 2, -sine, sine)
    for head in range(2):
        values = projected[:, head * HD:(head + 1) * HD] / spread * key_gain[head:head + 1, :]
        turned = values * cosine + pltpu.roll(values, HD // 2, 1) * sine
        keys_out[:, head * HD:(head + 1) * HD] = turned[0:KROWS].astype(jnp.bfloat16)

    run((2,), (0, 4))
    weights_rest()
    z_receive("A", 4)
    y_receive(4)
    run((1,), (1, 2))
    weights_far(0)
    for first in (0, 2):
        from_sibling(1, first, 2)
        from_sibling(2, first, 2)
    run((1,), (5, 6))
    y_finish(3)
    run((2,), (1, 2, 5, 6))
    run((3,), (0, 4, 1, 2, 5, 6))
    y_finish(4)
    weights_far(1)
    run((0,), (0, 4, 1, 2, 5, 6))
    run((0, 3, 2, 1), (3,))
    for q in (0, 2, 1, 3):
        from_sibling(3, q, 1)
    for p in (0, 3, 2, 1):
        chunk(p, 7)
        give(p)

    gathered[0] = acc[0, :, 0:ROWS]
    for d in range(1, NZ):
        receive(f"a{d}", gathered.at[NZ - d], up(d))
    stats = merged(*(gathered[:, i, :] for i in range(4)))
    for i in range(4):
        part[i:i + 1, :] = stats[i]
    part[4:8, :] = jnp.zeros((4, ROWS), jnp.float32)
    mine = c * NY + y
    for i, peer in enumerate(voc_peers):
        send(f"v{i + 1}", part, parts.at[mine], peer)
    for i, peer in enumerate(partners):
        send(f"u{i}", part, parts.at[8 + mine], peer)
    parts[mine] = part[...]

    def place(d):
        source = lax.rem(voc + 8 - d, 8)
        return lax.rem(source, 2) * NY + lax.div(source, 2)

    for d in range(1, 8):
        receive(f"v{d}", parts.at[place(d)], sibling)
    receive("g", partner_segments, sibling)
    for d in range(8):
        receive(f"u{d}", parts.at[8 + place(d)], sibling)

    lane = lax.broadcasted_iota(jnp.int32, (1, ROWS), 1)
    seat = lax.broadcasted_iota(jnp.int32, (8, ROWS), 0)
    totals = []
    for first, group, labels in ((0, grp, segments), (8, partner, partner_segments)):
        length = lengths[group]
        sums = jnp.zeros((8, ROWS), jnp.float32)
        counts = jnp.zeros((8, ROWS), jnp.float32)
        last = jnp.zeros((1, ROWS), jnp.float32)
        for half in range(2):
            start = first + half * NY
            top, expsum, moment, picked = merged(*(parts[start:start + NY, i, :] for i in range(4)))
            logsum = top + jnp.log(expsum)
            slot = lane + half * ROWS
            live = slot < length
            logprob = jnp.where(live, picked - logsum, 0.0)
            label = labels[half:half + 1, :]
            if first == 0:
                logprob_out[half:half + 1, :] = logprob
                entropy_out[half:half + 1, :] = jnp.where(live, logsum - moment / expsum, 0.0)
            last = last + jnp.where(slot == length - 1, label.astype(jnp.float32), 0.0)
            member = seat == jnp.where(live, label, SEGS)
            sums = sums + jnp.where(member, logprob, 0.0)
            counts = counts + jnp.where(member, 1.0, 0.0)
        totals.append((
            jnp.sum(sums, axis=1, keepdims=True), jnp.sum(counts, axis=1, keepdims=True),
            jnp.sum(last, axis=1, keepdims=True),
        ))
    (sums, counts, last), (got_sums, got_counts, _) = totals
    row = lax.broadcasted_iota(jnp.int32, (8, 1), 0).astype(jnp.float32)
    even = lax.rem(x, 2) == 0
    joined = continues[grp - lax.rem(grp, 2)] == 1
    got_last = jnp.max(jnp.where((got_counts > 0) & (row < SEGS), row, 0.0), axis=0, keepdims=True)
    source = jnp.where(even, 0.0, got_last)
    target = jnp.where(even, last, 0.0)
    extra_sum = jnp.sum(jnp.where(row == source, got_sums, 0.0), axis=0, keepdims=True)
    extra_count = jnp.sum(jnp.where(row == source, got_counts, 0.0), axis=0, keepdims=True)
    update = joined & (row == target)
    total_sum = sums + jnp.where(update, extra_sum, 0.0)
    total_count = counts + jnp.where(update, extra_count, 0.0)
    means = total_sum / jnp.maximum(total_count, 1.0)
    mean_out[...] = jnp.sum(jnp.where(seat == lane, means, 0.0), axis=0, keepdims=True)[:, 0:SEGS]
    for copy in sent:
        copy.wait_send()


MESSAGES = 128


def local(
    final_hidden, norm_gain, head_weight, token_ids, group_lengths, segment_ids, continues,
    layer_input, key_weight, key_gain, positions, key_rows,
):
    steps = np.arange(HD // 2, dtype=np.float64)
    freqs = np.exp(-(2.0 * steps / HD) * np.log(ROPE_BASE)).astype(np.float32)
    freqs = jnp.asarray(np.concatenate([freqs, freqs])[None, :])
    anywhere = pl.BlockSpec(memory_space=pl.ANY)
    vmem = pl.BlockSpec(memory_space=pltpu.VMEM)
    smem = pl.BlockSpec(memory_space=pltpu.SMEM)
    f32, bf16 = jnp.float32, jnp.bfloat16
    logprob, entropy, mean, keys = pl.pallas_call(
        kernel,
        out_shape=(
            jax.ShapeDtypeStruct((2, ROWS), f32),
            jax.ShapeDtypeStruct((2, ROWS), f32),
            jax.ShapeDtypeStruct((1, SEGS), f32),
            jax.ShapeDtypeStruct((KROWS, BOTH), bf16),
        ),
        in_specs=[anywhere] * 4 + [vmem, vmem, smem, vmem, smem, vmem, vmem, smem, vmem],
        out_specs=(vmem,) * 4,
        scratch_shapes=[
            pltpu.VMEM((ROWS, DIM), bf16),
            pltpu.VMEM((8, DIM, ROWS), bf16),
            pltpu.VMEM((8, WROWS, DIM), bf16),
            pltpu.VMEM((2 * ROWS, DIM), bf16),
            pltpu.VMEM((DIM, BOTH), bf16),
            pltpu.VMEM((4, 1, BOTH), jnp.int32),
            pltpu.VMEM((4, 8, BOTH), f32),
            pltpu.VMEM((8, 8, ROWS), f32),
            pltpu.VMEM((8, ROWS), f32),
            pltpu.VMEM((16, 8, ROWS), f32),
            pltpu.VMEM((KPAD, HD), f32),
            pltpu.VMEM((8, KPAD, HD), f32),
            pltpu.VMEM((2, ROWS), jnp.int32),
            pltpu.SemaphoreType.DMA((4,)),
            pltpu.SemaphoreType.DMA((MESSAGES,)),
            pltpu.SemaphoreType.DMA((MESSAGES,)),
        ],
        compiler_params=pltpu.CompilerParams(
            collective_id=0, has_side_effects=True, vmem_limit_bytes=62 * 2**20
        ),
    )(
        final_hidden, head_weight, layer_input, key_weight,
        norm_gain.reshape(DIM // HD, HD), token_ids.reshape(-1, ROWS), group_lengths,
        segment_ids.reshape(2, ROWS), continues, key_gain.reshape(2, HD),
        positions.reshape(2, ROWS), key_rows, freqs,
    )
    return (logprob.reshape(-1), entropy.reshape(-1), mean.reshape(-1), keys)


def solution(mesh):
    in_specs = (
        P("grp", None),
        P(),
        P(("vocab", "grp"), None),
        P(),
        P(),
        P("grp"),
        P(),
        P("grp", None),
        P(None, "vocab"),
        P("vocab"),
        P("grp"),
        P("grp"),
    )
    out_specs = (P("grp"), P("grp"), P("grp"), P("grp", "vocab"))
    return jax.shard_map(local, mesh=mesh, in_specs=in_specs, out_specs=out_specs, check_vma=False)
```

time: 82.4 us -> 63.2 us (0.77)
  Pallas kernels: 68.7 us -> 58.8 us
  local copies, waits for them, and re-layouts: 12.5 us -> 3.53 us
    pallas_call x1, Pallas kernels: 68.7 us -> 58.8 us  [local(): pl.pallas_call(kernel, out_shape=(jax.ShapeDtypeStruct((2, ROWS), f32), j...]
    unnamed x30 -> x8, local copies, waits for them, and re-layouts: 12.5 us -> 3.53 us
where the time goes in v2:
time: 63.2 us; the launch traced here: 63 us
  Pallas kernels  58.8 us (93%)
  local copies, waits for them, and re-layouts  3.53 us (6%)
  between operations  0.65 us (1%)
    pallas_call x1, Pallas kernels, local(): pl.pallas_call(kernel, out_shape=(jax.ShapeDtypeStruct((2, ROWS), f32), j...  58.8 us
    unnamed x8, local copies, waits for them, and re-layouts  3.53 us

profile of v2, /device:TPU:1, one launch (start us, length us, event | category | flops | bytes accessed | tf_op | source)
XLA Modules:
  0.0 63.0 jit_solution(3426839723954674411)
XLA Ops:
  0.6 58.8 %shard_map.156 = (f32[2,128]{1,0:T(2,128)}, f32[2,128]{1,0:T(2,128)}, f32[1,4]{1,0:T(1,128)}, bf16[25,256]{1,0:T(8,128)(2,1)}) custom-call(bf16[256,2048]{1,0:T(8,128)(2,1)} %hidden.1, bf16[196,2048]{1,0:T(8,128)(2,1)} %weight.1, bf16[256,2048]{1,0:T(8,128)(2,1)} %layer_input.1, bf16[2048,256]{1,0:T(8,128)(2,1)} %key_weight.1, f32[16,128]{1,0:T(8,128)} %bitcast.9, ...), custom_call_target="tpu_custom_call" | custom-call | tf_op jit(solution)/shard_map/pallas_call | solution.py:417
  59.5 0.0 copy-start
  59.5 1.2 %copy.21 = f32[256]{0:T(256)} copy(f32[256]{0:T(256)} %bitcast.11) | data formatting | bytes 2048
  60.7 0.0 copy-start.1
  60.7 1.2 %copy.22 = f32[256]{0:T(256)} copy(f32[256]{0:T(256)} %bitcast.10) | data formatting | bytes 2048
  61.9 0.0 copy-done.1
  61.9 0.5 copy.23
  62.4 0.0 copy-done
  62.4 0.6 copy.24
Async XLA Ops:
  59.5 2.9 %copy-start = (bf16[25,256]{1,0:T(8,128)(2,1)S(1)}, bf16[25,256]{1,0:T(8,128)(2,1)}, u32[]{:S(2)}) copy-start(bf16[25,256]{1,0:T(8,128)(2,1)} %get-tuple-element.19) | copy-start | bytes 38404
  60.7 1.2 %copy-start.1 = (f32[1,4]{1,0:T(1,128)S(1)}, f32[1,4]{1,0:T(1,128)}, u32[]{:S(2)}) copy-start(f32[1,4]{1,0:T(1,128)} %get-tuple-element.10) | copy-start | bytes 52

commit v3 on v2

--- a/solution.py
+++ b/solution.py
@@ -17,7 +17,7 @@
 DIM = 2048
 WROWS = 196
 WPIECE = DIM // 4
-SHARE = 352
+SHARE = 320
 ALONE = DIM - SHARE * NY
 KROWS = 25
 KPAD = 32
@@ -164,13 +164,15 @@
     def share(yy, first=0):
         return pl.multiple_of(ALONE + SHARE * lax.rem(yy, NY) + first, 16)
 
-    LAST = {("S", "+"): 3, ("S", "-"): 4, ("A", "+"): 4, ("A", "-"): 3}
+    LAST = {"S+": 3, "S-": 4, "A+": 4, "A-": 3, "B+": 4, "B-": 3}
 
     def away(way, k):
         return (NZ - k) % NZ if way == "+" else k
 
     def z_part(kind, d):
-        return features(d, 0, ALONE) if kind == "A" else features(d, share(y), SHARE)
+        if kind == "S":
+            return features(d, share(y), SHARE)
+        return features(d, 0 if kind == "A" else ALONE // 2, ALONE // 2)
 
     def z_send(kind, way, k):
         send(
@@ -180,11 +182,11 @@
 
     def z_receive(kind, k):
         for way in "+-":
-            if k > LAST[kind, way]:
+            if k > LAST[kind + way]:
                 continue
             d = away(way, k)
             receive(f"z{kind}{way}{k}", z_part(kind, d), up(1))
-            if k < LAST[kind, way]:
+            if k < LAST[kind + way]:
                 z_send(kind, way, k + 1)
         if kind == "S":
             ref = shares(k, share(y), SHARE)
@@ -210,9 +212,12 @@
         receive(f"yf+{k}", shares(k, share(y + 2), half_share), y_up)
         receive(f"yf-{k}", shares(k, share(y + 2, half_share), half_share), y_down)
 
-    for kind in "SA":
-        for way in "+-":
-            z_send(kind, way, 1)
+    def z_start(kinds):
+        for kind in kinds:
+            for way in "+-":
+                z_send(kind, way, 1)
+
+    z_start(FIRST)
     own_piece("+", 1, 1)
     own_piece("-", 3, 1)
     own_piece("+", 2, 2)
@@ -269,67 +274,62 @@
             if d:
                 send(f"a{d}", acc.at[p, :, pl.ds(half * ROWS, ROWS)], gathered.at[NZ - d], up(d))
 
-    z_receive("S", 1)
-    z_receive("A", 1)
-    z_receive("S", 2)
-    y_receive(1)
-
-    weights_near(0)
-    z_receive("A", 2)
-    z_receive("S", 3)
-    weights_near(1)
-    y_finish(1)
-    local_copies[1].wait()
-    receive("w0", wts.at[4], sibling)
-    run((1,), (0, 4))
-    y_receive(2)
-    z_receive("A", 3)
-    z_receive("S", 4)
-    y_finish(2)
-    y_receive(3)
-
-    for i in range(7):
-        receive(f"k{i + 1}", all_squares.at[i + 1], sibling)
-    square_sum = squares[...]
-    for i in range(7):
-        square_sum = square_sum + all_squares[i + 1]
-    spread = jnp.sqrt(square_sum / (HD * 16) + NORM_EPS)
-    places_row = jnp.concatenate([positions[0:1, :], positions[1:2, :]], axis=1).astype(jnp.float32)
-    places = jnp.sum(picks * places_row, axis=1, keepdims=True)
-    angles = places * freqs[0:1, :]
-    turns = jnp.floor(angles * (0.5 / np.pi) + 0.5)
-    angles = ((angles - turns * TWO_PI_1) - turns * TWO_PI_2) - turns * TWO_PI_3
-    lanes = lax.broadcasted_iota(jnp.int32, (KPAD, HD), 1)
-    cosine = jnp.cos(angles)
-    sine = jnp.sin(angles)
-    sine = jnp.where(lanes < HD // 2, -sine, sine)
-    for head in range(2):
-        values = projected[:, head * HD:(head + 1) * HD] / spread * key_gain[head:head + 1, :]
-        turned = values * cosine + pltpu.roll(values, HD // 2, 1) * sine
-        keys_out[:, head * HD:(head + 1) * HD] = turned[0:KROWS].astype(jnp.bfloat16)
-
-    run((2,), (0, 4))
-    weights_rest()
-    z_receive("A", 4)
-    y_receive(4)
-    run((1,), (1, 2))
-    weights_far(0)
-    for first in (0, 2):
-        from_sibling(1, first, 2)
-        from_sibling(2, first, 2)
-    run((1,), (5, 6))
-    y_finish(3)
-    run((2,), (1, 2, 5, 6))
-    run((3,), (0, 4, 1, 2, 5, 6))
-    y_finish(4)
-    weights_far(1)
-    run((0,), (0, 4, 1, 2, 5, 6))
-    run((0, 3, 2, 1), (3,))
-    for q in (0, 2, 1, 3):
-        from_sibling(3, q, 1)
-    for p in (0, 3, 2, 1):
+    def finish_keys():
+        for i in range(7):
+            receive(f"k{i + 1}", all_squares.at[i + 1], sibling)
+        square_sum = squares[...]
+        for i in range(7):
+            square_sum = square_sum + all_squares[i + 1]
+        spread = jnp.sqrt(square_sum / (HD * 16) + NORM_EPS)
+        places_row = jnp.concatenate([positions[0:1, :], positions[1:2, :]], axis=1).astype(jnp.float32)
+        places = jnp.sum(picks * places_row, axis=1, keepdims=True)
+        angles = places * freqs[0:1, :]
+        turns = jnp.floor(angles * (0.5 / np.pi) + 0.5)
+        angles = ((angles - turns * TWO_PI_1) - turns * TWO_PI_2) - turns * TWO_PI_3
+        lanes = lax.broadcasted_iota(jnp.int32, (KPAD, HD), 1)
+        cosine = jnp.cos(angles)
+        sine = jnp.sin(angles)
+        sine = jnp.where(lanes < HD // 2, -sine, sine)
+        for head in range(2):
+            values = projected[:, head * HD:(head + 1) * HD] / spread * key_gain[head:head + 1, :]
+            turned = values * cosine + pltpu.roll(values, HD // 2, 1) * sine
+            keys_out[:, head * HD:(head + 1) * HD] = turned[0:KROWS].astype(jnp.bfloat16)
+
+    def start_chunks():
+        local_copies[1].wait()
+        receive("w0", wts.at[4], sibling)
+
+    def near_from_sibling():
+        for first in (0, 2):
+            from_sibling(1, first, 2)
+            from_sibling(2, first, 2)
+
+    def far_from_sibling():
+        for q in (0, 2, 1, 3):
+            from_sibling(3, q, 1)
+
+    def last_chunk(p):
         chunk(p, 7)
         give(p)
+
+    marks = []
+
+    def settle():
+        for copy in sent[:marks[0]]:
+            copy.wait_send()
+        del sent[:marks[0]]
+
+    events = {
+        "M": lambda: marks.append(len(sent)), "w": settle,
+        "S": lambda k: z_receive("S", k), "A": lambda k: z_receive("A", k),
+        "B": lambda k: z_receive("B", k), "a": z_start,
+        "Y": y_receive, "F": y_finish, "K": finish_keys,
+        "n": weights_near, "r": weights_rest, "f": weights_far,
+        "o": start_chunks, "m": near_from_sibling, "l": far_from_sibling,
+        "C": run, "L": last_chunk,
+    }
+    for name, *rest in ORDER:
+        events[name](*rest)
 
     gathered[0] = acc[0, :, 0:ROWS]
     for d in range(1, NZ):
@@ -339,10 +339,10 @@
         part[i:i + 1, :] = stats[i]
     part[4:8, :] = jnp.zeros((4, ROWS), jnp.float32)
     mine = c * NY + y
-    for i, peer in enumerate(voc_peers):
-        send(f"v{i + 1}", part, parts.at[mine], peer)
-    for i, peer in enumerate(partners):
-        send(f"u{i}", part, parts.at[8 + mine], peer)
+    for d in (4, 3, 5, 2, 6, 0, 1, 7):
+        send(f"u{d}", part, parts.at[8 + mine], partners[d])
+        if d:
+            send(f"v{d}", part, parts.at[mine], voc_peers[d - 1])
     parts[mine] = part[...]
 
     def place(d):
@@ -401,6 +401,11 @@
 
 
 MESSAGES = 128
+MOST = (0, 4, 1, 2, 5, 6)
+FIRST = "SAB"
+ORDER = [("S", 1), ("A", 1), ("B", 1), ("S", 2), ("Y", 1), ("n", 0), ("A", 2), ("B", 2), ("S", 3), ("n", 1), ("F", 1),
+    ("o",), ("Y", 2), ("A", 3), ("B", 3), ("S", 4), ("C", (1,), (0, 4)), ("F", 2), ("Y", 3), ("C", (2,), (0, 4)), ("K",), ("r",), ("A", 4), ("B", 4), ("C", (1,), (1, 2)), ("Y", 4), ("m",), ("C", (1,), (5, 6)), ("C", (2,), (1, 2, 5, 6)), ("M",), ("f", 0), ("F", 3), ("C", (3,), MOST), ("w",), ("f", 1), ("C", (3, 2, 1), (3,)), ("F", 4), ("C", (0,), MOST), ("C", (0,), (3,)), ("l",), ("L", 0), ("L", 3), ("L", 2), ("L", 1),
+]
 
 
 def local(
@@ -451,6 +456,22 @@
         segment_ids.reshape(2, ROWS), continues, key_gain.reshape(2, HD),
         positions.reshape(2, ROWS), key_rows, freqs,
     )
+    outs = (logprob, entropy, mean, keys)
+
+    def finish(*refs):
+        copies = [pltpu.make_async_copy(refs[i], refs[4 + i], refs[8].at[i]) for i in range(4)]
+        for copy in copies:
+            copy.start()
+        for copy in copies:
+            copy.wait()
+
+    logprob, entropy, mean, keys = pl.pallas_call(
+        finish,
+        out_shape=tuple(jax.ShapeDtypeStruct(a.shape, a.dtype) for a in outs),
+        in_specs=[anywhere] * 4,
+        out_specs=(anywhere,) * 4,
+        scratch_shapes=[pltpu.SemaphoreType.DMA((4,))],
+    )(*outs)
     return (logprob.reshape(-1), entropy.reshape(-1), mean.reshape(-1), keys)
 
 

time: 63.2 us -> 60.1 us (0.951)
  local copies, waits for them, and re-layouts: 3.53 us -> 0 us
    unnamed x8 -> x0, local copies, waits for them, and re-layouts: 3.53 us -> none
    pallas_call x0 -> x1, Pallas kernels: none -> 1.71 us  [local(): pl.pallas_call(finish, out_shape=tuple((jax.ShapeDtypeStruct(a.shape, a.d...]
    pallas_call x1, Pallas kernels: 58.8 us -> 57.6 us  [local(): pl.pallas_call(kernel, out_shape=(jax.ShapeDtypeStruct((2, ROWS), f32), j...]
where the time goes in v3:
time: 60.1 us; the launch traced here: 60 us
  Pallas kernels  59.3 us (99%)
  between operations  0.64 us (1%)
    pallas_call x1, Pallas kernels, local(): pl.pallas_call(kernel, out_shape=(jax.ShapeDtypeStruct((2, ROWS), f32), j...  57.6 us
    pallas_call x1, Pallas kernels, local(): pl.pallas_call(finish, out_shape=tuple((jax.ShapeDtypeStruct(a.shape, a.d...  1.71 us

profile of v3, /device:TPU:1, one launch (start us, length us, event | category | flops | bytes accessed | tf_op | source)
XLA Modules:
  0.0 60.0 jit_solution(10448403613047722534)
XLA Ops:
  0.6 57.6 %shard_map.156 = (f32[2,128]{1,0:T(2,128)}, f32[2,128]{1,0:T(2,128)}, f32[1,4]{1,0:T(1,128)}, bf16[25,256]{1,0:T(8,128)(2,1)}) custom-call(bf16[256,2048]{1,0:T(8,128)(2,1)} %hidden.1, bf16[196,2048]{1,0:T(8,128)(2,1)} %weight.1, bf16[256,2048]{1,0:T(8,128)(2,1)} %layer_input.1, bf16[2048,256]{1,0:T(8,128)(2,1)} %key_weight.1, f32[16,128]{1,0:T(8,128)} %bitcast.9, ...), custom_call_target="tpu_custom_call" | custom-call | tf_op jit(solution)/shard_map/pallas_call | solution.py:422
  58.2 1.7 %shard_map.157 = (f32[2,128]{1,0:T(2,128)}, f32[2,128]{1,0:T(2,128)}, f32[1,4]{1,0:T(1,128)}, bf16[25,256]{1,0:T(8,128)(2,1)}) custom-call(f32[2,128]{1,0:T(2,128)} %get-tuple-element.12.refs_0_, f32[2,128]{1,0:T(2,128)} %get-tuple-element.13.refs_1_, f32[1,4]{1,0:T(1,128)} %get-tuple-element.14.refs_2_, bf16[25,256]{1,0:T(8,128)(2,1)} %get-tuple-element.15.refs_3_), custom_call_target="tpu_custom_call" | custom-call | tf_op jit(solution)/shard_map/pallas_call | solution.py:468

commit v4 on v3

--- a/solution.py
+++ b/solution.py
@@ -17,7 +17,7 @@
 DIM = 2048
 WROWS = 196
 WPIECE = DIM // 4
-SHARE = 320
+SHARE = 352
 ALONE = DIM - SHARE * NY
 KROWS = 25
 KPAD = 32
@@ -45,8 +45,9 @@
 
 def kernel(
     hidden, weight, layer_input, key_weight,
-    gain, tokens, lengths, segments, continues, key_gain, positions, key_rows, freqs,
-    logprob_out, entropy_out, mean_out, keys_out,
+    gain_in, tokens_in, segments_in, key_gain_in, positions_in, freqs_in, lengths, continues, key_rows,
+    logprob_to, entropy_to, mean_to, keys_to,
+    gain, tokens, segments, key_gain, positions, freqs, logprob_out, entropy_out, mean_out, keys_out,
     raw, held, wts, lin, kwt, toks, acc, gathered, part, parts,
     squares, all_squares, partner_segments,
     local_sems, send_sems, recv_sems,
@@ -95,15 +96,26 @@
         pltpu.make_async_copy(layer_input, lin, local_sems.at[2]),
         pltpu.make_async_copy(key_weight, kwt, local_sems.at[3]),
     ]
-    for copy in local_copies:
-        copy.start()
+    small = [
+        pltpu.make_async_copy(src, dst, local_sems.at[4 + i]) for i, (src, dst) in enumerate((
+            (gain_in, gain), (tokens_in, tokens), (segments_in, segments),
+            (key_gain_in, key_gain), (positions_in, positions), (freqs_in, freqs),
+        ))
+    ]
+    results = [
+        pltpu.make_async_copy(src, dst, local_sems.at[10 + i]) for i, (src, dst) in enumerate((
+            (logprob_out, logprob_to), (entropy_out, entropy_to), (mean_out, mean_to), (keys_out, keys_to),
+        ))
+    ]
 
     barrier = pltpu.get_barrier_semaphore()
     partners = [(partner, lax.rem(voc + d, 8)) for d in range(8)]
     other_x = device(lax.rem(x + 3 + 2 * lax.rem(x, 2), NX), y, z, c)
-    peers = [up(d) for d in range(1, NZ)] + voc_peers + partners + [other_x]
+    peers = [other_x] + partners + [up(d) for d in (1, 7, 2, 6, 3, 5, 4)] + voc_peers
     for peer in peers:
         pl.semaphore_signal(barrier, inc=1, device_id=peer, device_id_type=MESH)
+    for copy in local_copies[:1] + small + local_copies[1:]:
+        copy.start()
     pl.semaphore_wait(barrier, len(peers))
 
     def piece(q):
@@ -149,6 +161,7 @@
         to_sibling(3, i + 2, 1)
 
     local_copies[0].wait()
+    small[0].wait()
     total = jnp.zeros((ROWS, HD), jnp.float32)
     for j in range(DIM // HD):
         block = raw[:, j * HD:(j + 1) * HD].astype(jnp.float32)
@@ -223,6 +236,8 @@
     own_piece("+", 2, 2)
     own_piece("-", 0, 2)
     send("w0", weight, wts.at[4], sibling)
+    for copy in small[1:]:
+        copy.wait()
     send("g", segments, partner_segments, partners[0])
 
     row_ids = lax.broadcasted_iota(jnp.int32, (KPAD, BOTH), 0)
@@ -294,6 +309,8 @@
             values = projected[:, head * HD:(head + 1) * HD] / spread * key_gain[head:head + 1, :]
             turned = values * cosine + pltpu.roll(values, HD // 2, 1) * sine
             keys_out[:, head * HD:(head + 1) * HD] = turned[0:KROWS].astype(jnp.bfloat16)
+
+        results[3].start()
 
     def start_chunks():
         local_copies[1].wait()
@@ -396,15 +413,19 @@
     total_count = counts + jnp.where(update, extra_count, 0.0)
     means = total_sum / jnp.maximum(total_count, 1.0)
     mean_out[...] = jnp.sum(jnp.where(seat == lane, means, 0.0), axis=0, keepdims=True)[:, 0:SEGS]
+    for copy in results[:3]:
+        copy.start()
     for copy in sent:
         copy.wait_send()
+    for copy in results:
+        copy.wait()
 
 
 MESSAGES = 128
 MOST = (0, 4, 1, 2, 5, 6)
 FIRST = "SAB"
-ORDER = [("S", 1), ("A", 1), ("B", 1), ("S", 2), ("Y", 1), ("n", 0), ("A", 2), ("B", 2), ("S", 3), ("n", 1), ("F", 1),
-    ("o",), ("Y", 2), ("A", 3), ("B", 3), ("S", 4), ("C", (1,), (0, 4)), ("F", 2), ("Y", 3), ("C", (2,), (0, 4)), ("K",), ("r",), ("A", 4), ("B", 4), ("C", (1,), (1, 2)), ("Y", 4), ("m",), ("C", (1,), (5, 6)), ("C", (2,), (1, 2, 5, 6)), ("M",), ("f", 0), ("F", 3), ("C", (3,), MOST), ("w",), ("f", 1), ("C", (3, 2, 1), (3,)), ("F", 4), ("C", (0,), MOST), ("C", (0,), (3,)), ("l",), ("L", 0), ("L", 3), ("L", 2), ("L", 1),
+ORDER = [("S", 1), ("A", 1), ("B", 1), ("S", 2), ("Y", 1), ("n", 0), ("A", 2), ("B", 2), ("S", 3), ("n", 1), ("K",), ("F", 1),
+    ("o",), ("Y", 2), ("A", 3), ("B", 3), ("S", 4), ("C", (1,), (0, 4)), ("F", 2), ("Y", 3), ("C", (2,), (0, 4)), ("r",), ("A", 4), ("B", 4), ("C", (1,), (1, 2)), ("Y", 4), ("m",), ("C", (1,), (5, 6)), ("C", (2,), (1, 2, 5, 6)), ("M",), ("f", 0), ("F", 3), ("C", (3,), MOST), ("w",), ("f", 1), ("C", (3, 2, 1), (3,)), ("F", 4), ("C", (0,), MOST), ("C", (0,), (3,)), ("l",), ("L", 0), ("L", 3), ("L", 2), ("L", 1),
 ]
 
 
@@ -416,7 +437,6 @@
     freqs = np.exp(-(2.0 * steps / HD) * np.log(ROPE_BASE)).astype(np.float32)
     freqs = jnp.asarray(np.concatenate([freqs, freqs])[None, :])
     anywhere = pl.BlockSpec(memory_space=pl.ANY)
-    vmem = pl.BlockSpec(memory_space=pltpu.VMEM)
     smem = pl.BlockSpec(memory_space=pltpu.SMEM)
     f32, bf16 = jnp.float32, jnp.bfloat16
     logprob, entropy, mean, keys = pl.pallas_call(
@@ -427,9 +447,19 @@
             jax.ShapeDtypeStruct((1, SEGS), f32),
             jax.ShapeDtypeStruct((KROWS, BOTH), bf16),
         ),
-        in_specs=[anywhere] * 4 + [vmem, vmem, smem, vmem, smem, vmem, vmem, smem, vmem],
-        out_specs=(vmem,) * 4,
+        in_specs=[anywhere] * 10 + [smem] * 3,
+        out_specs=(anywhere,) * 4,
         scratch_shapes=[
+            pltpu.VMEM((DIM // HD, HD), f32),
+            pltpu.VMEM((64, ROWS), jnp.int32),
+            pltpu.VMEM((2, ROWS), jnp.int32),
+            pltpu.VMEM((2, HD), f32),
+            pltpu.VMEM((2, ROWS), jnp.int32),
+            pltpu.VMEM((1, HD), f32),
+            pltpu.VMEM((2, ROWS), f32),
+            pltpu.VMEM((2, ROWS), f32),
+            pltpu.VMEM((1, SEGS), f32),
+            pltpu.VMEM((KROWS, BOTH), bf16),
             pltpu.VMEM((ROWS, DIM), bf16),
             pltpu.VMEM((8, DIM, ROWS), bf16),
             pltpu.VMEM((8, WROWS, DIM), bf16),
@@ -443,7 +473,7 @@
             pltpu.VMEM((KPAD, HD), f32),
             pltpu.VMEM((8, KPAD, HD), f32),
             pltpu.VMEM((2, ROWS), jnp.int32),
-            pltpu.SemaphoreType.DMA((4,)),
+            pltpu.SemaphoreType.DMA((14,)),
             pltpu.SemaphoreType.DMA((MESSAGES,)),
             pltpu.SemaphoreType.DMA((MESSAGES,)),
         ],
@@ -452,9 +482,8 @@
         ),
     )(
         final_hidden, head_weight, layer_input, key_weight,
-        norm_gain.reshape(DIM // HD, HD), token_ids.reshape(-1, ROWS), group_lengths,
-        segment_ids.reshape(2, ROWS), continues, key_gain.reshape(2, HD),
-        positions.reshape(2, ROWS), key_rows, freqs,
+        norm_gain.reshape(DIM // HD, HD), token_ids.reshape(-1, ROWS), segment_ids.reshape(2, ROWS),
+        key_gain.reshape(2, HD), positions.reshape(2, ROWS), freqs, group_lengths, continues, key_rows,
     )
     outs = (logprob, entropy, mean, keys)
 

time: 60.1 us -> 59.5 us (0.990)
  no operation moved by 1% of the time
where the time goes in v4:
time: 59.5 us; the launch traced here: 59.4 us
  Pallas kernels  58.8 us (99%)
  between operations  0.64 us (1%)
    pallas_call x1, Pallas kernels, local(): pl.pallas_call(kernel, out_shape=(jax.ShapeDtypeStruct((2, ROWS), f32), j...  57.1 us
    pallas_call x1, Pallas kernels, local(): pl.pallas_call(finish, out_shape=tuple((jax.ShapeDtypeStruct(a.shape, a.d...  1.71 us

profile of v4, /device:TPU:1, one launch (start us, length us, event | category | flops | bytes accessed | tf_op | source)
XLA Modules:
  0.0 59.4 jit_solution(18200613423214021352)
XLA Ops:
  0.6 57.1 %shard_map.156 = (f32[2,128]{1,0:T(2,128)}, f32[2,128]{1,0:T(2,128)}, f32[1,4]{1,0:T(1,128)}, bf16[25,256]{1,0:T(8,128)(2,1)}) custom-call(bf16[256,2048]{1,0:T(8,128)(2,1)} %hidden.1, bf16[196,2048]{1,0:T(8,128)(2,1)} %weight.1, bf16[256,2048]{1,0:T(8,128)(2,1)} %layer_input.1, bf16[2048,256]{1,0:T(8,128)(2,1)} %key_weight.1, f32[16,128]{1,0:T(8,128)} %bitcast.9, ...), custom_call_target="tpu_custom_call" | custom-call | tf_op jit(solution)/shard_map/pallas_call | solution.py:442
  57.7 1.7 %shard_map.157 = (f32[2,128]{1,0:T(2,128)}, f32[2,128]{1,0:T(2,128)}, f32[1,4]{1,0:T(1,128)}, bf16[25,256]{1,0:T(8,128)(2,1)}) custom-call(f32[2,128]{1,0:T(2,128)} %get-tuple-element.12.refs_0_, f32[2,128]{1,0:T(2,128)} %get-tuple-element.13.refs_1_, f32[1,4]{1,0:T(1,128)} %get-tuple-element.14.refs_2_, bf16[25,256]{1,0:T(8,128)(2,1)} %get-tuple-element.15.refs_3_), custom_call_target="tpu_custom_call" | custom-call | tf_op jit(solution)/shard_map/pallas_call | solution.py:497

commit v5 on v4

--- a/solution.py
+++ b/solution.py
@@ -395,6 +395,9 @@
             member = seat == jnp.where(live, label, SEGS)
             sums = sums + jnp.where(member, logprob, 0.0)
             counts = counts + jnp.where(member, 1.0, 0.0)
+        if first == 0:
+            for copy in results[:2]:
+                copy.start()
         totals.append((
             jnp.sum(sums, axis=1, keepdims=True), jnp.sum(counts, axis=1, keepdims=True),
             jnp.sum(last, axis=1, keepdims=True),
@@ -413,8 +416,7 @@
     total_count = counts + jnp.where(update, extra_count, 0.0)
     means = total_sum / jnp.maximum(total_count, 1.0)
     mean_out[...] = jnp.sum(jnp.where(seat == lane, means, 0.0), axis=0, keepdims=True)[:, 0:SEGS]
-    for copy in results[:3]:
-        copy.start()
+    results[2].start()
     for copy in sent:
         copy.wait_send()
     for copy in results:

time: 59.5 us -> 59.5 us (level)
  no operation moved by 1% of the time
where the time goes in v5:
time: 59.5 us; the launch traced here: 59.4 us
  Pallas kernels  58.8 us (99%)
  between operations  0.64 us (1%)
    pallas_call x1, Pallas kernels, local(): pl.pallas_call(kernel, out_shape=(jax.ShapeDtypeStruct((2, ROWS), f32), j...  57.1 us
    pallas_call x1, Pallas kernels, local(): pl.pallas_call(finish, out_shape=tuple((jax.ShapeDtypeStruct(a.shape, a.d...  1.71 us

profile of v5, /device:TPU:1, one launch (start us, length us, event | category | flops | bytes accessed | tf_op | source)
XLA Modules:
  0.0 59.4 jit_solution(18200613423214021352)
XLA Ops:
  0.6 57.1 %shard_map.156 = (f32[2,128]{1,0:T(2,128)}, f32[2,128]{1,0:T(2,128)}, f32[1,4]{1,0:T(1,128)}, bf16[25,256]{1,0:T(8,128)(2,1)}) custom-call(bf16[256,2048]{1,0:T(8,128)(2,1)} %hidden.1, bf16[196,2048]{1,0:T(8,128)(2,1)} %weight.1, bf16[256,2048]{1,0:T(8,128)(2,1)} %layer_input.1, bf16[2048,256]{1,0:T(8,128)(2,1)} %key_weight.1, f32[16,128]{1,0:T(8,128)} %bitcast.9, ...), custom_call_target="tpu_custom_call" | custom-call | tf_op jit(solution)/shard_map/pallas_call | solution.py:444
  57.7 1.7 %shard_map.157 = (f32[2,128]{1,0:T(2,128)}, f32[2,128]{1,0:T(2,128)}, f32[1,4]{1,0:T(1,128)}, bf16[25,256]{1,0:T(8,128)(2,1)}) custom-call(f32[2,128]{1,0:T(2,128)} %get-tuple-element.12.refs_0_, f32[2,128]{1,0:T(2,128)} %get-tuple-element.13.refs_1_, f32[1,4]{1,0:T(1,128)} %get-tuple-element.14.refs_2_, bf16[25,256]{1,0:T(8,128)(2,1)} %get-tuple-element.15.refs_3_), custom_call_target="tpu_custom_call" | custom-call | tf_op jit(solution)/shard_map/pallas_call | solution.py:499
